TPU v7x, 32 devices: a whole 2x2x4 slice. The times are simulated.
32 devices in a mesh: dp: 2 (over x), space: 16 (over z, y, core).
Axes of the slice: x: 2, y: 2, z: 4, core: 2. Of those that a mesh axis runs over, the one named last changes fastest.
Arguments:
- stash: bfloat16 [16, 16, 4, 8640], P('space', None, 'dp'), may hold values from -5 to 5
- piece_map: int32 [16, 16], P(None, 'space'), may hold values from 0 to 15, as said below
- gain_one: float32 [768], replicated, may hold values from 0.5 to 1.5
- spec_one: float32 [2, 8, 96, 96], replicated, may hold values from -0.4375 to 0.4375
- bias_one: float32 [2, 768], replicated, may hold values from -3 to 3
- spec_two: float32 [2, 8, 96, 96], replicated, may hold values from -0.4375 to 0.4375
- bias_two: float32 [2, 768], replicated, may hold values from -0.6 to 0.6
- gain_two: float32 [768], replicated, may hold values from 0.5 to 1.5
- fc_one: bfloat16 [768, 3072], replicated, may hold values from -0.21875 to 0.21875
- bias_fc: float32 [3072], replicated, may hold values from -3 to 3
- fc_two: bfloat16 [3072, 768], replicated, may hold values from -0.109375 to 0.109375
- cotangent: bfloat16 [4, 16, 180, 768], P('dp', 'space'), may hold values from -6 to 6
Outputs:
- grad_input: float32 [4, 16, 180, 768], P('dp', 'space')
- grad_fc_one: float32 [768, 3072], P(None, ('dp', 'space'))
- grad_fc_two: float32 [3072, 768], P(('dp', 'space'))
- grad_bias_fc: float32 [3072], replicated
- grad_bias_out: float32 [768], replicated
- grad_gain_one: float32 [768], replicated
- grad_gain_two: float32 [768], replicated
- grad_spec_one: float32 [2, 8, 96, 96], replicated
- grad_bias_one: float32 [2, 768], replicated
- grad_spec_two: float32 [2, 8, 96, 96], replicated
- grad_bias_two: float32 [2, 768], replicated
Inputs may be any that keep to these rules, and one draw needn't show every extreme that they name: `piece_map`: each column holds every number from 0 to 15 once.
All inputs are finite; a program needn't handle non-finite values.
Results may differ from a plain program's by a relative error of at most 0.0046.
Values may be sent and summed in bfloat16 or wider, within the bound.
A program may use at most 128 MiB of HBM per device.

v0:
```python
import math

import jax
import jax.numpy as jnp
from jax import lax
from jax.sharding import PartitionSpec as P

KW = 64


epsilon = 1e-05
highest = lax.Precision.HIGHEST


def layer_norm(values, gain_vector):
    centred = values - jnp.mean(values, axis=-1, keepdims=True)
    spread = jnp.mean(centred * centred, axis=-1, keepdims=True)
    return centred * lax.rsqrt(spread + epsilon) * gain_vector


def smooth_gate(values):
    return jax.nn.gelu(values, approximate=True)


def block_mix(real_part, imag_part, weights, biases):
    blocks = weights.shape[1]
    width_block = weights.shape[2]
    leading = real_part.shape[:-1]
    real_blocks = real_part.reshape(leading + (blocks, width_block))
    imag_blocks = imag_part.reshape(leading + (blocks, width_block))
    bias_real = biases[0].reshape(blocks, width_block)
    bias_imag = biases[1].reshape(blocks, width_block)
    new_real = (
        jnp.einsum("...ni,nio->...no", real_blocks, weights[0], precision=highest)
        - jnp.einsum("...ni,nio->...no", imag_blocks, weights[1], precision=highest)
        + bias_real
    )
    new_imag = (
        jnp.einsum("...ni,nio->...no", real_blocks, weights[1], precision=highest)
        + jnp.einsum("...ni,nio->...no", imag_blocks, weights[0], precision=highest)
        + bias_imag
    )
    return (
        new_real.reshape(leading + (blocks * width_block,)),
        new_imag.reshape(leading + (blocks * width_block,)),
    )


def spectral_mlp(spec_real, spec_imag, spec_one, bias_one, spec_two, bias_two):
    inner_real, inner_imag = block_mix(spec_real, spec_imag, spec_one, bias_one)
    return block_mix(smooth_gate(inner_real), smooth_gate(inner_imag), spec_two, bias_two)


def wave_tables(length, total_modes):
    positions = jnp.arange(length, dtype=jnp.int32)
    frequency = jnp.arange(total_modes, dtype=jnp.int32)
    phases = positions[:, None] * frequency[None, :] % length
    angles = phases.astype(jnp.float32) * (2.0 * math.pi / length)
    factor = 1.0 / math.sqrt(length)
    return (jnp.cos(angles) * factor, jnp.sin(angles) * factor)


def meridian_apply(table, field):
    return jnp.einsum("hk,bhmd->bkmd", table, field, precision=highest)


def meridian_forward(real_part, imag_part, merid_cos, merid_sin):
    new_real = meridian_apply(merid_cos, real_part) + meridian_apply(merid_sin, imag_part)
    new_imag = meridian_apply(merid_cos, imag_part) - meridian_apply(merid_sin, real_part)
    return (new_real, new_imag)


def meridian_inverse(real_part, imag_part, merid_cos, merid_sin):
    new_real = meridian_apply(merid_cos, real_part) - meridian_apply(merid_sin, imag_part)
    new_imag = meridian_apply(merid_cos, imag_part) + meridian_apply(merid_sin, real_part)
    return (new_real, new_imag)


def zonal_project(field, table):
    return jnp.einsum("brwd,wk->brkd", field, table, precision=highest)


def zonal_expand(field, table):
    return jnp.einsum("brkd,wk->brwd", field, table, precision=highest)


def local(
    stash,
    piece_map,
    gain_one,
    spec_one,
    bias_one,
    spec_two,
    bias_two,
    gain_two,
    fc_one,
    bias_fc,
    fc_two,
    cotangent,
):
    samples, lat_rows, lon_cells, model_width = cotangent.shape
    space_ranks = lax.axis_size("space")
    lat_total = lat_rows * space_ranks
    tokens = samples * lat_rows * lon_cells
    arrived = lax.all_to_all(stash, "space", split_axis=1, concat_axis=0, tiled=True)
    ordering = jnp.argsort(piece_map[:, 0])
    placed = jnp.take(arrived[:, 0], ordering, axis=0)
    inputs = jnp.transpose(placed, (1, 0, 2)).reshape(samples, lat_rows, lon_cells, model_width)
    base_field = inputs.astype(jnp.float32)
    zonal_cos, zonal_sin = wave_tables(lon_cells, KW)
    doubling = jnp.where(jnp.arange(KW) == 0, 1.0, 2.0).astype(jnp.float32)
    back_cos = zonal_cos * doubling
    back_sin = zonal_sin * doubling
    merid_cos, merid_sin = wave_tables(lat_total, lat_total)
    normed, pull_one = jax.vjp(layer_norm, base_field, gain_one)
    zonal_real = zonal_project(normed, zonal_cos)
    zonal_imag = -zonal_project(normed, zonal_sin)
    modes_real, modes_imag = (
        lax.all_to_all(zonal_real, "space", split_axis=2, concat_axis=1, tiled=True),
        lax.all_to_all(zonal_imag, "space", split_axis=2, concat_axis=1, tiled=True),
    )
    spec_real, spec_imag = meridian_forward(modes_real, modes_imag, merid_cos, merid_sin)
    mixed_spec, pull_mix = jax.vjp(
        spectral_mlp, spec_real, spec_imag, spec_one, bias_one, spec_two, bias_two
    )
    back_real, back_imag = meridian_inverse(mixed_spec[0], mixed_spec[1], merid_cos, merid_sin)
    rows_real, rows_imag = (
        lax.all_to_all(back_real, "space", split_axis=1, concat_axis=2, tiled=True),
        lax.all_to_all(back_imag, "space", split_axis=1, concat_axis=2, tiled=True),
    )
    spatial = zonal_expand(rows_real, back_cos) - zonal_expand(rows_imag, back_sin)
    mixed_field = base_field + normed + spatial
    normed_two, pull_two = jax.vjp(layer_norm, mixed_field, gain_two)
    normed_flat = normed_two.astype(jnp.bfloat16).reshape(tokens, model_width)
    hidden_pre = jnp.dot(normed_flat, fc_one, preferred_element_type=jnp.float32) + bias_fc
    active, pull_gate = jax.vjp(smooth_gate, hidden_pre)
    active_flat = active.astype(jnp.bfloat16)
    upstream = cotangent.reshape(tokens, model_width)
    grad_active = jnp.einsum("td,fd->tf", upstream, fc_two, preferred_element_type=jnp.float32)
    grad_hidden = pull_gate(grad_active)[0]
    grad_hidden_flat = grad_hidden.astype(jnp.bfloat16)
    grad_normed_two = jnp.einsum(
        "tf,df->td", grad_hidden_flat, fc_one, preferred_element_type=jnp.float32
    )
    term_one = jnp.einsum(
        "td,tf->df", normed_flat, grad_hidden_flat, preferred_element_type=jnp.float32
    )
    term_two = jnp.einsum("td,tf->df", upstream, active_flat, preferred_element_type=jnp.float32)
    grad_mixed_norm, grad_gain_two = pull_two(grad_normed_two.reshape(mixed_field.shape))
    grad_mixed = cotangent.astype(jnp.float32) + grad_mixed_norm
    grad_back_real = zonal_project(grad_mixed, back_cos)
    grad_back_imag = -zonal_project(grad_mixed, back_sin)
    grad_modes_real, grad_modes_imag = (
        lax.all_to_all(grad_back_real, "space", split_axis=2, concat_axis=1, tiled=True),
        lax.all_to_all(grad_back_imag, "space", split_axis=2, concat_axis=1, tiled=True),
    )
    grad_out_real, grad_out_imag = meridian_forward(
        grad_modes_real, grad_modes_imag, merid_cos, merid_sin
    )
    pulled = pull_mix((grad_out_real, grad_out_imag))
    grad_merid_real, grad_merid_imag = meridian_inverse(pulled[0], pulled[1], merid_cos, merid_sin)
    grad_rows_real, grad_rows_imag = (
        lax.all_to_all(grad_merid_real, "space", split_axis=1, concat_axis=2, tiled=True),
        lax.all_to_all(grad_merid_imag, "space", split_axis=1, concat_axis=2, tiled=True),
    )
    grad_normed = (
        grad_mixed
        + zonal_expand(grad_rows_real, zonal_cos)
        - zonal_expand(grad_rows_imag, zonal_sin)
    )
    grad_base, grad_gain_one = pull_one(grad_normed)
    grad_input = grad_mixed + grad_base
    bias_sum = jnp.sum(grad_hidden, axis=0)
    out_sum = jnp.sum(cotangent, axis=(0, 1, 2), dtype=jnp.float32)
    totals = lax.psum(
        (
            grad_gain_one,
            grad_gain_two,
            pulled[2],
            pulled[3],
            pulled[4],
            pulled[5],
            bias_sum,
            out_sum,
        ),
        ("dp", "space"),
    )
    paired = (
        lax.psum_scatter(term_one, "dp", scatter_dimension=1, tiled=True),
        lax.psum_scatter(term_two, "dp", scatter_dimension=1, tiled=True),
    )
    summed = (
        lax.psum_scatter(paired[0], "space", scatter_dimension=1, tiled=True),
        lax.psum_scatter(paired[1], "space", scatter_dimension=1, tiled=True),
    )
    grad_scale = 1.0 / math.sqrt(samples * lax.axis_size("dp") * lat_total * lon_cells)
    return (
        grad_input,
        summed[0] * grad_scale,
        (summed[1] * grad_scale).T,
        totals[6] * grad_scale,
        totals[7] * grad_scale,
        totals[0] * grad_scale,
        totals[1] * grad_scale,
        totals[2] * grad_scale,
        totals[3] * grad_scale,
        totals[4] * grad_scale,
        totals[5] * grad_scale,
    )


def solution(mesh):
    placed = (
        P("space", None, "dp", None),
        P(None, "space"),
        P(),
        P(),
        P(),
        P(),
        P(),
        P(),
        P(),
        P(),
        P(),
        P("dp", "space", None, None),
    )
    return jax.shard_map(
        local,
        mesh=mesh,
        in_specs=placed,
        out_specs=(
            P("dp", "space", None, None),
            P(None, ("dp", "space")),
            P(("dp", "space"), None),
            P(),
            P(),
            P(),
            P(),
            P(),
            P(),
            P(),
            P(),
        ),
        check_vma=False,
    )
```

profile of v0, /device:TPU:0, one launch (start us, length us, event | category | flops | bytes accessed | tf_op | source)
XLA Modules:
  0.0 540.7 jit_solution(15111530025571040540)
XLA Ops:
  8.0 7.4 %all-to-all-start = ((bf16[1,16,2,8640]{3,2,0,1:T(2,128)(2,1)}), bf16[1,16,2,8640]{3,2,0,1:T(2,128)(2,1)S(1)}, u32[]{:S(2)}, u32[]{:S(2)}) async-start(bf16[1,16,2,8640]{3,2,0,1:T(2,128)(2,1)} %bitcast.441), calls=%async_computation | async-start | bytes 1114112 | tf_op jit(solution)/shard_map/all_to_all | solution.py:105
  15.5 1.9 sort.17
  17.4 12.9 %all-to-all-done = bf16[1,16,2,8640]{3,2,0,1:T(2,128)(2,1)S(1)} async-done(((bf16[1,16,2,8640]{3,2,0,1:T(2,128)(2,1)}), bf16[1,16,2,8640]{3,2,0,1:T(2,128)(2,1)S(1)}, u32[]{:S(2)}, u32[]{:S(2)}) %all-to-all-start) | async-done | bytes 552992 | tf_op jit(solution)/shard_map/all_to_all | solution.py:105
  30.2 1.7 gather_fusion
  37.2 4.3 all-to-all-start.1
  43.9 9.8 %all-to-all-done.1 = f32[2,1,64,768]{3,0,1,2:T(2,128)S(1)} async-done(((f32[2,1,64,768]{3,0,1,2:T(2,128)}), f32[2,1,64,768]{3,0,1,2:T(2,128)S(1)}, u32[]{:S(2)}, u32[]{:S(2)}) %all-to-all-start.1) | async-done | bytes 393248 | tf_op jit(solution)/shard_map/all_to_all | solution.py:119
  53.7 3.7 all-to-all-start.2
  59.2 10.4 %all-to-all-done.2 = f32[2,1,64,768]{3,0,1,2:T(2,128)S(1)} async-done(((f32[2,1,64,768]{3,0,1,2:T(2,128)}), f32[2,1,64,768]{3,0,1,2:T(2,128)S(1)}, u32[]{:S(2)}, u32[]{:S(2)}) %all-to-all-start.2) | async-done | bytes 393248 | tf_op jit(solution)/shard_map/all_to_all | solution.py:120
  70.9 1.7 fusion.28
  73.6 1.5 fusion.106
  79.8 1.6 fusion.111
  84.0 1.8 fusion.19
  88.4 3.8 all-to-all-start.3
  95.2 9.1 %all-to-all-done.3 = f32[2,16,4,768]{3,2,0,1:T(4,128)S(1)} async-done(((f32[2,16,4,768]{3,2,0,1:T(4,128)}), f32[2,16,4,768]{3,2,0,1:T(4,128)S(1)}, u32[]{:S(2)}, u32[]{:S(2)}) %all-to-all-start.3) | async-done | bytes 393248 | tf_op jit(solution)/shard_map/all_to_all | solution.py:128
  104.3 3.6 all-to-all-start.4
  107.9 6.3 %fusion.368 = f32[360,3072]{1,0:T(8,128)} fusion(bf16[360,768]{1,0:T(8,128)(2,1)S(1)} %copy-done.24, bf16[3072,768]{1,0:T(8,128)(2,1)} %param.22), kind=kOutput, calls=%fused_computation.459 | convolution fusion | flops 1698693120 | bytes 9695232 | tf_op jit(solution)/shard_map/td,fd->tf/dot_general | solution.py:139
  114.5 1.3 fusion.131
  115.8 4.2 all-to-all-done.4
  120.2 1.6 fusion.365
  123.2 9.3 %fusion.363 = (f32[3072]{0:T(1024)S(1)}, bf16[360,3072]{1,0:T(8,128)(2,1)S(1)}, f32[360,3072]{1,0:T(8,128)}) fusion(f32[360,3072]{1,0:T(8,128)} %fusion.368, f32[3072]{0:T(1024)S(1)} %copy-done.30, bf16[360,768]{1,0:T(8,128)(2,1)S(1)} %reshape.380, bf16[768,3072]{1,0:T(8,128)(2,1)} %param.20), kind=kOutput, calls=%fused_computation.455 | convolution fusion | flops 1723020288 | bytes 16355328 | tf_op jit(solution)/shard_map/dot_general | solution.py:135
  132.5 1.4 copy-done.17
  134.0 5.1 fusion.32
  140.1 8.9 %convolution_bitcast_fusion = f32[768,3072]{0,1:T(8,128)} fusion(bf16[360,768]{1,0:T(8,128)(2,1)S(1)} %copy-done.25, f32[360,3072]{1,0:T(8,128)} %get-tuple-element.83), kind=kOutput, calls=%fused_computation.3 | convolution fusion | flops 1708646400 | bytes 14413824 | tf_op jit(solution)/shard_map/td,tf->df/dot_general | solution.py:148
  149.0 6.0 %fusion.34 = f32[360,768]{1,0:T(8,128)} fusion(bf16[768,3072]{1,0:T(8,128)(2,1)} %param.20, bf16[360,3072]{1,0:T(8,128)(2,1)} %copy-done.17), kind=kOutput, calls=%fused_computation.86 | convolution fusion | flops 1698693120 | bytes 8036352 | tf_op jit(solution)/shard_map/tf,df->td/dot_general | solution.py:142
  155.0 1.4 reshape.381
  158.4 1.7 convert_reduce_fusion
  162.2 3.7 all-to-all-start.6
  168.1 10.0 %all-to-all-done.6 = f32[2,1,64,768]{3,0,1,2:T(2,128)S(1)} async-done(((f32[2,1,64,768]{3,0,1,2:T(2,128)}), f32[2,1,64,768]{3,0,1,2:T(2,128)S(1)}, u32[]{:S(2)}, u32[]{:S(2)}) %all-to-all-start.6) | async-done | bytes 393248 | tf_op jit(solution)/shard_map/all_to_all | solution.py:154
  178.1 3.6 all-to-all-start.5
  183.3 10.6 %all-to-all-done.5 = f32[2,1,64,768]{3,0,1,2:T(2,128)S(1)} async-done(((f32[2,1,64,768]{3,0,1,2:T(2,128)}), f32[2,1,64,768]{3,0,1,2:T(2,128)S(1)}, u32[]{:S(2)}, u32[]{:S(2)}) %all-to-all-start.5) | async-done | bytes 393248 | tf_op jit(solution)/shard_map/all_to_all | solution.py:155
  193.8 1.6 fusion.366
  197.1 1.3 fusion.367
  199.8 2.0 fusion.87
  216.5 33.5 %reduce-scatter.9.cloned.1.call-done = f32[768,1536]{1,0:T(8,128)} async-done(((f32[768,3072]{1,0:T(8,128)}), f32[768,1536]{1,0:T(8,128)}) %reduce-scatter.9.cloned.1.call-update) | async-done | bytes 4718608 | tf_op jit(solution)/shard_map/reduce_scatter | solution.py:189
  250.0 6.1 %copy.208 = f32[768,1536]{0,1:T(8,128)} copy(f32[768,1536]{1,0:T(8,128)} %reduce-scatter.9.cloned.1.call-done) | data formatting | bytes 9437184
  256.2 108.3 %reduce-scatter.11.cloned.1.call-done = f32[768,1536]{0,1:T(8,128)} async-done(((f32[768,3072]{0,1:T(8,128)}), f32[768,1536]{0,1:T(8,128)}) %reduce-scatter.11.cloned.1.call-update) | async-done | bytes 4718608 | tf_op jit(solution)/shard_map/reduce_scatter | solution.py:190
  365.6 1.9 fusion.124
  370.8 1.9 fusion.118
  378.0 5.6 %all-to-all-start.8 = ((f32[2,16,4,768]{3,2,0,1:T(4,128)}), f32[2,16,4,768]{3,2,0,1:T(4,128)S(1)}, u32[]{:S(2)}, u32[]{:S(2)}) async-start(f32[2,16,4,768]{3,2,0,1:T(4,128)} %copy.176), calls=%async_computation.8 | async-start | bytes 786432 | tf_op jit(solution)/shard_map/all_to_all | solution.py:164
  385.6 10.2 %all-to-all-done.8 = f32[2,16,4,768]{3,2,0,1:T(4,128)S(1)} async-done(((f32[2,16,4,768]{3,2,0,1:T(4,128)}), f32[2,16,4,768]{3,2,0,1:T(4,128)S(1)}, u32[]{:S(2)}, u32[]{:S(2)}) %all-to-all-start.8) | async-done | bytes 393248 | tf_op jit(solution)/shard_map/all_to_all | solution.py:164
  395.9 4.0 all-to-all-start.7
  400.2 43.3 %all-reduce.16.cloned.1.call-done = (f32[2,8,96,96]{3,2,1,0:T(8,128)}, f32[2,8,96,96]{3,2,1,0:T(8,128)}) async-done(((f32[2,8,96,96]{3,2,1,0:T(8,128)}, f32[2,8,96,96]{3,2,1,0:T(8,128)}), (f32[2,8,96,96]{3,2,1,0:T(8,128)}, f32[2,8,96,96]{3,2,1,0:T(8,128)})) %all-reduce.16.cloned.1.call-update) | async-done | bytes 1179664 | tf_op jit(solution)/shard_map/psum | solution.py:175
  443.5 2.7 broadcast_multiply_fusion
  446.5 1.3 convolution_bitcast_fusion.1
  447.9 1.7 multiply_reduce_fusion.2
  450.6 2.1 copy.188
  452.8 41.9 %all-reduce.12 = (f32[3072]{0:T(1024)S(1)}, f32[768]{0:T(1024)S(1)}, f32[768]{0:T(1024)S(1)}, f32[768]{0:T(1024)S(1)}, f32[2,768]{1,0:T(2,128)S(1)}, /*index=5*/f32[2,768]{1,0:T(2,128)S(1)}) all-reduce(f32[3072]{0:T(1024)S(1)} %get-tuple-element.73, ...), channel_id=1, replica_groups=mesh['dp'=2,'space'=16] {'dp','space'}, use_global_device_ids=true, to_apply=%region_14.15 | all-reduce | flops 8448 | bytes 67584 | tf_op jit(solution)/shard_map/psum | solution.py:175
  499.1 32.0 %reduce-scatter.15.cloned.1.call-done = f32[96,768]{1,0:T(8,128)} async-done(((f32[1536,768]{1,0:T(8,128)}), f32[96,768]{1,0:T(8,128)}) %reduce-scatter.15.cloned.1.call-update) | async-done | bytes 294928
  (186 shorter events, 72.4 us)
Async XLA Ops:
  8.0 22.2 %all-to-all-start = ((bf16[1,16,2,8640]{3,2,0,1:T(2,128)(2,1)}), bf16[1,16,2,8640]{3,2,0,1:T(2,128)(2,1)S(1)}, u32[]{:S(2)}, u32[]{:S(2)}) async-start(bf16[1,16,2,8640]{3,2,0,1:T(2,128)(2,1)} %bitcast.441), calls=%async_computation | async-start | bytes 1114112 | tf_op jit(solution)/shard_map/all_to_all | solution.py:105
  34.3 0.7 copy-start.26
  37.2 16.5 %all-to-all-start.1 = ((f32[2,1,64,768]{3,0,1,2:T(2,128)}), f32[2,1,64,768]{3,0,1,2:T(2,128)S(1)}, u32[]{:S(2)}, u32[]{:S(2)}) async-start(f32[2,1,64,768]{3,0,1,2:T(2,128)} %copy.140), calls=%async_computation.1 | async-start | bytes 786432 | tf_op jit(solution)/shard_map/all_to_all | solution.py:119
  42.8 14.6 %copy-start.28 = (f32[2,768]{1,0:T(2,128)S(1)}, f32[2,768]{1,0:T(2,128)}, u32[]{:S(2)}) copy-start(f32[2,768]{1,0:T(2,128)} %param.16) | copy-start | bytes 18436
  42.9 14.8 %copy-start.29 = (f32[2,768]{1,0:T(2,128)S(1)}, f32[2,768]{1,0:T(2,128)}, u32[]{:S(2)}) copy-start(f32[2,768]{1,0:T(2,128)} %param.18) | copy-start | bytes 18436
  53.7 15.8 %all-to-all-start.2 = ((f32[2,1,64,768]{3,0,1,2:T(2,128)}), f32[2,1,64,768]{3,0,1,2:T(2,128)S(1)}, u32[]{:S(2)}, u32[]{:S(2)}) async-start(f32[2,1,64,768]{3,0,1,2:T(2,128)} %copy.142), calls=%async_computation.2 | async-start | bytes 786432 | tf_op jit(solution)/shard_map/all_to_all | solution.py:120
  70.9 1.9 copy-start.5
  72.9 2.1 copy-start.1
  72.9 2.1 copy-start.23
  76.4 1.3 copy-start.22
  77.7 3.7 copy-start.3
  77.7 1.3 copy-start.14
  79.0 2.4 copy-start.20
  82.1 1.3 copy-start.7
  82.9 1.1 copy-start.15
  86.9 5.3 copy-start.18
  88.4 15.9 %all-to-all-start.3 = ((f32[2,16,4,768]{3,2,0,1:T(4,128)}), f32[2,16,4,768]{3,2,0,1:T(4,128)S(1)}, u32[]{:S(2)}, u32[]{:S(2)}) async-start(f32[2,16,4,768]{3,2,0,1:T(4,128)} %copy.152), calls=%async_computation.3 | async-start | bytes 786432 | tf_op jit(solution)/shard_map/all_to_all | solution.py:128
  94.2 13.7 %copy-start.24 = (bf16[360,768]{1,0:T(8,128)(2,1)S(1)}, bf16[360,768]{1,0:T(8,128)(2,1)}, u32[]{:S(2)}) copy-start(bf16[360,768]{1,0:T(8,128)(2,1)} %reshape.373) | copy-start | bytes 1658884
  104.3 15.7 %all-to-all-start.4 = ((f32[2,16,4,768]{3,2,0,1:T(4,128)}), f32[2,16,4,768]{3,2,0,1:T(4,128)S(1)}, u32[]{:S(2)}, u32[]{:S(2)}) async-start(f32[2,16,4,768]{3,2,0,1:T(4,128)} %copy.155), calls=%async_computation.4 | async-start | bytes 786432 | tf_op jit(solution)/shard_map/all_to_all | solution.py:129
  107.8 142.1 %reduce-scatter.9.cloned.1.call-start = ((), (), s32[]{:S(2)}) async-start(), calls=%async_computation.13 | async-start | bytes 14155776 | tf_op jit(solution)/shard_map/reduce_scatter | solution.py:189
  121.8 0.7 copy-start.27
  122.5 0.7 copy-start.30
  132.5 1.5 copy-start.17
  139.1 1.1 copy-start.25
  139.1 225.4 %reduce-scatter.11.cloned.1.call-start = ((), (), s32[]{:S(2)}) async-start(), calls=%async_computation.14 | async-start | bytes 14155776 | tf_op jit(solution)/shard_map/reduce_scatter | solution.py:190
  156.3 1.0 copy-start
  157.3 1.1 copy-start.19
  162.2 15.9 %all-to-all-start.6 = ((f32[2,1,64,768]{3,0,1,2:T(2,128)}), f32[2,1,64,768]{3,0,1,2:T(2,128)S(1)}, u32[]{:S(2)}, u32[]{:S(2)}) async-start(f32[2,1,64,768]{3,0,1,2:T(2,128)} %copy.160), calls=%async_computation.6 | async-start | bytes 786432 | tf_op jit(solution)/shard_map/all_to_all | solution.py:154
  178.1 15.7 %all-to-all-start.5 = ((f32[2,1,64,768]{3,0,1,2:T(2,128)}), f32[2,1,64,768]{3,0,1,2:T(2,128)S(1)}, u32[]{:S(2)}, u32[]{:S(2)}) async-start(f32[2,1,64,768]{3,0,1,2:T(2,128)} %copy.158), calls=%async_computation.5 | async-start | bytes 786432 | tf_op jit(solution)/shard_map/all_to_all | solution.py:155
  181.7 261.8 %all-reduce.16.cloned.1.call-start = ((), (), s32[]{:S(2)}) async-start(), calls=%async_computation.17 | async-start | bytes 3145728 | tf_op jit(solution)/shard_map/psum | solution.py:175
  198.4 3.4 copy-start.8
  199.7 2.1 copy-start.13
  199.7 2.1 copy-start.16
  201.8 1.3 copy-start.2
  203.1 2.3 copy-start.9
  203.1 1.2 copy-start.4
  204.3 1.9 copy-start.21
  207.3 2.1 copy-start.10
  216.5 280.6 %reduce-scatter.13.cloned.1.call-start = ((), (), s32[]{:S(2)}) async-start(), calls=%async_computation.15 | async-start | bytes 5013504
  256.1 275.0 %reduce-scatter.15.cloned.1.call-start = ((), (), s32[]{:S(2)}) async-start(), calls=%async_computation.16 | async-start | bytes 5013504
  364.5 1.1 copy-start.6
  365.6 1.9 copy-start.11
  370.7 1.9 copy-start.12
  378.0 17.9 %all-to-all-start.8 = ((f32[2,16,4,768]{3,2,0,1:T(4,128)}), f32[2,16,4,768]{3,2,0,1:T(4,128)S(1)}, u32[]{:S(2)}, u32[]{:S(2)}) async-start(f32[2,16,4,768]{3,2,0,1:T(4,128)} %copy.176), calls=%async_computation.8 | async-start | bytes 786432 | tf_op jit(solution)/shard_map/all_to_all | solution.py:164
  395.9 50.4 %all-to-all-start.7 = ((f32[2,16,4,768]{3,2,0,1:T(4,128)}), f32[2,16,4,768]{3,2,0,1:T(4,128)S(1)}, u32[]{:S(2)}, u32[]{:S(2)}) async-start(f32[2,16,4,768]{3,2,0,1:T(4,128)} %copy.173), calls=%async_computation.7 | async-start | bytes 786432 | tf_op jit(solution)/shard_map/all_to_all | solution.py:163
Sparse Core Ops, SparseCore 0:
  139.2 110.7 reduce-scatter.8
  252.3 112.1 reduce-scatter.10
  368.3 83.4 reduce-scatter.12
  455.5 75.5 reduce-scatter.14
Sparse Core Ops, SparseCore 1:
  216.6 226.8 all-reduce.15
where the time goes:
time: 549 us; the launch traced here: 541 us
  waiting for transfers between devices  294 us (54%)
  matrix products  88.4 us (16%)
  local copies, waits for them, and re-layouts  44.1 us (8%)
  blocking collectives  41.9 us (8%)
  starting transfers between devices  40.5 us (7%)
  between operations  16.6 us (3%)
  other arithmetic  14.9 us (3%)
    reduce_scatter x1, waiting for transfers between devices, local(): lax.psum_scatter(term_two, 'dp', scatter_dimension=1, tiled=True)  108 us
    psum x1, waiting for transfers between devices, local(): lax.psum((grad_gain_one, grad_gain_two, pulled[2], pulled[3], pulled[4],...  43.3 us
    psum x1, blocking collectives, local(): lax.psum((grad_gain_one, grad_gain_two, pulled[2], pulled[3], pulled[4],...  41.9 us
    reduce_scatter x1, waiting for transfers between devices, local(): lax.psum_scatter(term_one, 'dp', scatter_dimension=1, tiled=True)  33.5 us
    unnamed x7, waiting for transfers between devices  32.1 us
    unnamed x69, local copies, waits for them, and re-layouts  19.2 us
    dot_general x16, matrix products, meridian_apply(): return jnp.einsum('hk,bhmd->bkmd', table, field, precision=highest)  14.6 us
    all_to_all x1, waiting for transfers between devices, local(): lax.all_to_all(stash, 'space', split_axis=1, concat_axis=0, tiled=True)  12.9 us
  transfers between devices with their start and end apart: 14, of which 12 were waited for; matrix products, arithmetic and copies ran while one was open for 18% of the time, Pallas kernels for 0%

commit v1 on v0

v1 whole, which is shorter than its diff:
```python
import math

import jax
import jax.numpy as jnp
import numpy as np
from jax import lax
from jax.sharding import PartitionSpec as P

KW = 64


epsilon = 1e-05
high = lax.Precision.HIGH
everyone = ("dp", "space")


def layer_norm(values, gain_vector):
    centred = values - jnp.mean(values, axis=-1, keepdims=True)
    spread = jnp.mean(centred * centred, axis=-1, keepdims=True)
    return centred * lax.rsqrt(spread + epsilon) * gain_vector


def smooth_gate(values):
    return jax.nn.gelu(values, approximate=True)


def complex_blocks(weights):
    top = jnp.concatenate((weights[0], weights[1]), axis=2)
    bottom = jnp.concatenate((-weights[1], weights[0]), axis=2)
    return jnp.concatenate((top, bottom), axis=1)


def complex_bias(biases, blocks):
    return biases.reshape(2, blocks, 1, -1).transpose(1, 2, 0, 3).reshape(blocks, 1, -1)


def block_dot(values, weights):
    return jnp.einsum("nri,nio->nro", values, weights, precision=high)


def spectral_mlp(spectrum, spec_one, bias_one, spec_two, bias_two):
    blocks = spec_one.shape[1]
    inner = block_dot(spectrum, complex_blocks(spec_one)) + complex_bias(bias_one, blocks)
    return block_dot(smooth_gate(inner), complex_blocks(spec_two)) + complex_bias(bias_two, blocks)


def zonal_tables(length, ranks):
    positions = np.arange(length)[:, None]
    frequency = np.arange(KW)[None, :]
    angles = (positions * frequency % length) * (2.0 * math.pi / length)
    table = np.stack((np.cos(angles), -np.sin(angles))) / math.sqrt(length)
    doubled = table * np.where(frequency == 0, 1.0, 2.0)
    shaped = [
        item.reshape(2, length, ranks, KW // ranks).transpose(1, 2, 0, 3).astype(np.float32)
        for item in (table, doubled)
    ]
    return shaped


def meridian_table(length, ranks):
    positions = np.arange(length)
    angles = (positions[:, None] * positions[None, :] % length) * (2.0 * math.pi / length)
    cosine = np.cos(angles) / math.sqrt(length)
    sine = np.sin(angles) / math.sqrt(length)
    table = np.stack((np.stack((cosine, -sine), -1), np.stack((sine, cosine), -1)), 1)
    return table.reshape(ranks, length // ranks, 2, length, 2).astype(np.float32)


def swap(pieces):
    return lax.all_to_all(pieces, "space", split_axis=0, concat_axis=0, tiled=True)


def to_modes(field, zonal, merid, blocks, carried):
    pieces = jnp.einsum("brwd,wscm->sbrcmd", field, zonal, precision=high)
    modes = swap(pieces.astype(carried)).astype(jnp.float32)
    spectrum = jnp.einsum("lbrcmd,lrcke->bmked", modes, merid, precision=high)
    rows = math.prod(spectrum.shape[:3])
    split = spectrum.reshape(rows, 2, blocks, -1)
    return split.transpose(2, 0, 1, 3).reshape(blocks, rows, -1)


def from_modes(spectrum, zonal, merid, samples, width, carried):
    blocks, rows = spectrum.shape[:2]
    length = merid.shape[3]
    split = spectrum.reshape(blocks, rows, 2, -1).transpose(1, 2, 0, 3)
    shaped = split.reshape(samples, rows // (samples * length), length, 2, width)
    pieces = jnp.einsum("bmked,lrcke->lbrcmd", shaped, merid, precision=high)
    modes = swap(pieces.astype(carried)).astype(jnp.float32)
    return jnp.einsum("sbrcmd,wscm->brwd", modes, zonal, precision=high)


def local(
    stash,
    piece_map,
    gain_one,
    spec_one,
    bias_one,
    spec_two,
    bias_two,
    gain_two,
    fc_one,
    bias_fc,
    fc_two,
    cotangent,
):
    samples, lat_rows, lon_cells, model_width = cotangent.shape
    space_ranks = lax.axis_size("space")
    lat_total = lat_rows * space_ranks
    tokens = samples * lat_rows * lon_cells
    blocks = spec_one.shape[1]
    arrived = lax.all_to_all(stash, "space", split_axis=1, concat_axis=0, tiled=True)
    ordering = jnp.argsort(piece_map[:, 0])
    placed = jnp.take(arrived[:, 0], ordering, axis=0)
    inputs = jnp.transpose(placed, (1, 0, 2)).reshape(samples, lat_rows, lon_cells, model_width)
    base_field = inputs.astype(jnp.float32)
    zonal, zonal_back = zonal_tables(lon_cells, space_ranks)
    merid = meridian_table(lat_total, space_ranks)
    normed, pull_one = jax.vjp(layer_norm, base_field, gain_one)
    spectrum = to_modes(normed, zonal, merid, blocks, jnp.float32)
    mixed_spec, pull_mix = jax.vjp(spectral_mlp, spectrum, spec_one, bias_one, spec_two, bias_two)
    spatial = from_modes(
        mixed_spec, zonal_back, merid, samples, model_width, jnp.float32
    )
    mixed_field = base_field + normed + spatial
    normed_two, pull_two = jax.vjp(layer_norm, mixed_field, gain_two)
    normed_flat = normed_two.astype(jnp.bfloat16).reshape(tokens, model_width)
    hidden_pre = jnp.dot(normed_flat, fc_one, preferred_element_type=jnp.float32) + bias_fc
    active, pull_gate = jax.vjp(smooth_gate, hidden_pre)
    active_flat = active.astype(jnp.bfloat16)
    upstream = cotangent.reshape(tokens, model_width)
    term_two = jnp.einsum("tf,td->fd", active_flat, upstream, preferred_element_type=jnp.float32)
    part_two = lax.psum_scatter(
        term_two.astype(jnp.bfloat16), everyone, scatter_dimension=0, tiled=True
    )
    grad_active = jnp.einsum("td,fd->tf", upstream, fc_two, preferred_element_type=jnp.float32)
    grad_hidden = pull_gate(grad_active)[0]
    grad_hidden_flat = grad_hidden.astype(jnp.bfloat16)
    term_one = jnp.einsum(
        "tf,td->fd", grad_hidden_flat, normed_flat, preferred_element_type=jnp.float32
    )
    part_one = lax.psum_scatter(
        term_one.astype(jnp.bfloat16), everyone, scatter_dimension=0, tiled=True
    )
    grad_normed_two = jnp.einsum(
        "tf,df->td", grad_hidden_flat, fc_one, preferred_element_type=jnp.float32
    )
    grad_mixed_norm, grad_gain_two = pull_two(grad_normed_two.reshape(mixed_field.shape))
    grad_mixed = cotangent.astype(jnp.float32) + grad_mixed_norm
    grad_spectrum = to_modes(grad_mixed, zonal_back, merid, blocks, jnp.bfloat16)
    pulled = pull_mix(grad_spectrum)
    grad_normed = grad_mixed + from_modes(
        pulled[0], zonal, merid, samples, model_width, jnp.bfloat16
    )
    grad_base, grad_gain_one = pull_one(grad_normed)
    grad_input = grad_mixed + grad_base
    bias_sum = jnp.sum(grad_hidden, axis=0)
    out_sum = jnp.sum(cotangent, axis=(0, 1, 2), dtype=jnp.float32)
    totals = lax.psum(
        (
            grad_gain_one,
            grad_gain_two,
            pulled[1],
            pulled[2],
            pulled[3],
            pulled[4],
            bias_sum,
            out_sum,
        ),
        everyone,
    )
    grad_scale = 1.0 / math.sqrt(samples * lax.axis_size("dp") * lat_total * lon_cells)
    return (
        grad_input,
        (part_one.astype(jnp.float32) * grad_scale).T,
        part_two.astype(jnp.float32) * grad_scale,
        totals[6] * grad_scale,
        totals[7] * grad_scale,
        totals[0] * grad_scale,
        totals[1] * grad_scale,
        totals[2] * grad_scale,
        totals[3] * grad_scale,
        totals[4] * grad_scale,
        totals[5] * grad_scale,
    )


def solution(mesh):
    placed = (
        P("space", None, "dp", None),
        P(None, "space"),
        P(),
        P(),
        P(),
        P(),
        P(),
        P(),
        P(),
        P(),
        P(),
        P("dp", "space", None, None),
    )
    return jax.shard_map(
        local,
        mesh=mesh,
        in_specs=placed,
        out_specs=(
            P("dp", "space", None, None),
            P(None, ("dp", "space")),
            P(("dp", "space"), None),
            P(),
            P(),
            P(),
            P(),
            P(),
            P(),
            P(),
            P(),
        ),
        check_vma=False,
    )
```

time: 549 us -> 521 us (0.949)
  matrix products: 88.4 us -> 59.3 us
  starting transfers between devices: 40.5 us -> 22.7 us
  waiting for transfers between devices: 294 us -> 310 us
  blocking collectives: 41.9 us -> 57.3 us
  local copies, waits for them, and re-layouts: 44.1 us -> 31.9 us
    psum x1, waiting for transfers between devices: 43.3 us -> 101 us  [local(): lax.psum((grad_gain_one, grad_gain_two, pulled[1], pulled[2], pulled[3],...]
    all_to_all x8 -> x3, waiting for transfers between devices: 64.3 us -> 23.1 us  [swap(): lax.all_to_all(pieces, 'space', split_axis=0, concat_axis=0, tiled=True)]
    unnamed x7 -> x3, waiting for transfers between devices: 32.1 us -> 0.05 us
    reduce_scatter x2, waiting for transfers between devices: 142 us -> 173 us  [the longest x1 111 us: local(): lax.psum_scatter(term_two.astype(jnp.bfloat16), everyone, scatter_dimensi...]
    dot_general x50 -> x16, matrix products: 66.8 us -> 37.8 us  [the longest x6 14.6 us: block_dot(): return jnp.einsum('nri,nio->nro', values, weights, precision=high)]
    all_to_all x8 -> x3, starting transfers between devices: 32.3 us -> 14.8 us  [swap(): lax.all_to_all(pieces, 'space', split_axis=0, concat_axis=0, tiled=True)]
    all_to_all x0 -> x1, blocking collectives: none -> 17.5 us  [swap(): lax.all_to_all(pieces, 'space', split_axis=0, concat_axis=0, tiled=True)]
    unnamed x69 -> x68, local copies, waits for them, and re-layouts: 19.2 us -> 9.9 us
  transfers between devices with their start and end apart: 14 -> 7, of which waited for: 12 -> 6; matrix products, arithmetic and copies ran while one was open for 18% -> 11% of each run, Pallas kernels for 0% -> 0%
where the time goes in v1:
time: 521 us; the launch traced here: 515 us
  waiting for transfers between devices  310 us (60%)
  matrix products  59.3 us (11%)
  blocking collectives  57.3 us (11%)
  local copies, waits for them, and re-layouts  31.9 us (6%)
  starting transfers between devices  22.7 us (4%)
  other arithmetic  19.5 us (4%)
  between operations  14.6 us (3%)
    reduce_scatter x1, waiting for transfers between devices, local(): lax.psum_scatter(term_two.astype(jnp.bfloat16), everyone, scatter_dimensi...  111 us
    psum x1, waiting for transfers between devices, local(): lax.psum((grad_gain_one, grad_gain_two, pulled[1], pulled[2], pulled[3],...  101 us
    reduce_scatter x1, waiting for transfers between devices, local(): lax.psum_scatter(term_one.astype(jnp.bfloat16), everyone, scatter_dimensi...  62 us
    psum x1, blocking collectives, local(): lax.psum((grad_gain_one, grad_gain_two, pulled[1], pulled[2], pulled[3],...  39.8 us
    all_to_all x3, waiting for transfers between devices, swap(): lax.all_to_all(pieces, 'space', split_axis=0, concat_axis=0, tiled=True)  23.1 us
    all_to_all x1, blocking collectives, swap(): lax.all_to_all(pieces, 'space', split_axis=0, concat_axis=0, tiled=True)  17.5 us
    all_to_all x3, starting transfers between devices, swap(): lax.all_to_all(pieces, 'space', split_axis=0, concat_axis=0, tiled=True)  14.8 us
    dot_general x6, matrix products, block_dot(): return jnp.einsum('nri,nio->nro', values, weights, precision=high)  14.6 us
  transfers between devices with their start and end apart: 7, of which 6 were waited for; matrix products, arithmetic and copies ran while one was open for 11% of the time, Pallas kernels for 0%

profile of v1, /device:TPU:0, one launch (start us, length us, event | category | flops | bytes accessed | tf_op | source)
XLA Modules:
  0.0 514.9 jit_solution(12274644097293364253)
XLA Ops:
  7.2 7.4 %all-to-all-start = ((bf16[1,16,2,8640]{3,2,0,1:T(2,128)(2,1)}), bf16[1,16,2,8640]{3,2,0,1:T(2,128)(2,1)S(1)}, u32[]{:S(2)}, u32[]{:S(2)}) async-start(bf16[1,16,2,8640]{3,2,0,1:T(2,128)(2,1)} %bitcast.227), calls=%async_computation | async-start | bytes 1114112 | tf_op jit(solution)/shard_map/all_to_all | solution.py:111
  14.6 1.9 sort.17
  16.5 12.9 %all-to-all-done = bf16[1,16,2,8640]{3,2,0,1:T(2,128)(2,1)S(1)} async-done(((bf16[1,16,2,8640]{3,2,0,1:T(2,128)(2,1)}), bf16[1,16,2,8640]{3,2,0,1:T(2,128)(2,1)S(1)}, u32[]{:S(2)}, u32[]{:S(2)}) %all-to-all-start) | async-done | bytes 552992 | tf_op jit(solution)/shard_map/all_to_all | solution.py:111
  29.4 1.7 gather_fusion
  35.0 1.5 copy.105
  36.5 5.0 all-to-all-start.1
  42.1 0.9 copy.158
  43.0 1.9 fusion.71
  44.9 1.2 copy.161
  46.1 0.9 copy.160
  48.6 11.5 %all-to-all-done.1 = f32[16,2,1,2,4,768]{5,1,4,3,2,0:T(2,128)S(1)} async-done(((f32[16,2,1,2,4,768]{5,1,4,3,2,0:T(2,128)}), f32[16,2,1,2,4,768]{5,1,4,3,2,0:T(2,128)S(1)}, u32[]{:S(2)}, u32[]{:S(2)}) %all-to-all-start.1) | async-done | bytes 786464 | tf_op jit(solution)/shard_map/all_to_all | solution.py:70
  62.0 2.6 convolution_add_fusion.2
  64.7 1.4 convolution_add_fusion.1
  67.7 1.4 copy.118
  69.1 5.6 %all-to-all-start.2 = ((f32[16,2,1,2,4,768]{5,4,1,3,2,0:T(4,128)}), f32[16,2,1,2,4,768]{5,4,1,3,2,0:T(4,128)}, u32[]{:S(2)}, u32[]{:S(2)}) async-start(f32[16,2,1,2,4,768]{5,4,1,3,2,0:T(4,128)} %copy.118), calls=%async_computation.2 | async-start | bytes 1572864 | tf_op jit(solution)/shard_map/all_to_all | solution.py:70
  75.1 6.7 %fusion.75 = f32[360,3072]{1,0:T(8,128)} fusion(bf16[360,768]{1,0:T(8,128)(2,1)S(1)} %reshape.326, bf16[3072,768]{1,0:T(8,128)(2,1)} %param.30), kind=kOutput, calls=%fused_computation.144 | convolution fusion | flops 1698693120 | bytes 9695232 | tf_op jit(solution)/shard_map/td,fd->tf/dot_general | solution.py:135
  81.8 11.6 %all-to-all-done.2 = f32[16,2,1,2,4,768]{5,4,1,3,2,0:T(4,128)} async-done(((f32[16,2,1,2,4,768]{5,4,1,3,2,0:T(4,128)}), f32[16,2,1,2,4,768]{5,4,1,3,2,0:T(4,128)}, u32[]{:S(2)}, u32[]{:S(2)}) %all-to-all-start.2) | async-done | bytes 786464 | tf_op jit(solution)/shard_map/all_to_all | solution.py:70
  93.4 2.4 fusion.73
  97.2 9.6 %fusion.68 = (f32[3072]{0:T(1024)S(1)}, bf16[360,3072]{1,0:T(8,128)(2,1)S(1)}, f32[360,3072]{1,0:T(8,128)}) fusion(f32[360,3072]{1,0:T(8,128)} %fusion.75, f32[3072]{0:T(1024)S(1)} %copy-done.27, bf16[360,768]{1,0:T(8,128)(2,1)S(1)} %reshape.337, bf16[768,3072]{1,0:T(8,128)(2,1)} %param.28), kind=kOutput, calls=%fused_computation.138 | convolution fusion | flops 1723020288 | bytes 16355328 | tf_op jit(solution)/shard_map/dot_general | solution.py:127
  106.9 1.4 copy-done.30
  108.3 5.2 %fusion.23 = f32[360,768]{1,0:T(8,128)} fusion(bf16[768,3072]{1,0:T(8,128)(2,1)} %param.28, bf16[360,3072]{1,0:T(8,128)(2,1)S(1)} %get-tuple-element.70), kind=kOutput, calls=%fused_computation.58 | convolution fusion | flops 1698693120 | bytes 8036352 | tf_op jit(solution)/shard_map/tf,df->td/dot_general | solution.py:144
  113.5 1.4 reshape.338
  115.9 1.7 fusion.70
  118.6 17.5 %all_to_all.29 = bf16[16,2,1,2,4,768]{5,4,3,1,2,0:T(4,128)(2,1)S(1)} all-to-all(bf16[16,2,1,2,4,768]{5,4,3,1,2,0:T(4,128)(2,1)S(1)} %copy.120), channel_id=1, replica_groups=mesh['dp'=2,'space'=16] {'space'}, dimensions={0} | all-to-all | bytes 786432 | tf_op jit(solution)/shard_map/all_to_all | solution.py:70
  136.5 0.9 copy.122
  137.5 1.6 reshape.342
  139.1 1.3 copy.123
  140.4 4.4 fusion.74
  144.7 0.9 fusion.47
  147.9 1.0 pad_add_fusion
  148.9 1.0 pad_add_fusion.1
  150.0 6.5 %convolution_convert_fusion.1 = bf16[3072,768]{1,0:T(8,128)(2,1)} fusion(bf16[360,768]{1,0:T(8,128)(2,1)} %copy-done.15, bf16[360,3072]{1,0:T(8,128)(2,1)} %copy-done.30), kind=kOutput, calls=%fused_computation.4 | convolution fusion | flops 1701052416 | bytes 7483392 | tf_op jit(solution)/shard_map/tf,td->fd/dot_general | solution.py:138
  156.8 7.6 %convolution_convert_fusion = bf16[3072,768]{1,0:T(8,128)(2,1)} fusion(bf16[360,768]{1,0:T(8,128)(2,1)} %copy-done.14, f32[360,3072]{1,0:T(8,128)} %get-tuple-element.89), kind=kOutput, calls=%fused_computation.3 | convolution fusion | flops 1711005696 | bytes 9695232 | tf_op jit(solution)/shard_map/tf,td->fd/dot_general | solution.py:131
  164.4 4.6 fusion.21
  169.0 2.4 copy.126
  171.4 2.5 reshape.345
  173.9 1.7 fusion.14
  175.6 1.0 copy.129
  176.6 4.2 all-to-all-start.4
  181.2 100.9 %all-reduce.12.cloned.1.call-done = (f32[2,8,96,96]{3,2,1,0:T(8,128)}, f32[2,8,96,96]{3,2,1,0:T(8,128)}) async-done(((f32[2,8,96,96]{3,2,1,0:T(8,128)}, f32[2,8,96,96]{3,2,1,0:T(8,128)}), (f32[2,8,96,96]{3,2,1,0:T(8,128)}, f32[2,8,96,96]{3,2,1,0:T(8,128)})) %all-reduce.12.cloned.1.call-update) | async-done | bytes 1179664 | tf_op jit(solution)/shard_map/psum | solution.py:158
  282.1 2.7 broadcast_multiply_fusion
  284.8 2.0 multiply_reduce_fusion.2
  288.0 2.1 copy.132
  290.1 39.8 %all-reduce.8 = (f32[3072]{0:T(1024)S(1)}, f32[768]{0:T(1024)S(1)}, f32[768]{0:T(1024)S(1)}, f32[768]{0:T(1024)S(1)}, f32[2,768]{1,0:T(2,128)S(1)}, /*index=5*/f32[2,768]{1,0:T(2,128)S(1)}) all-reduce(f32[3072]{0:T(1024)S(1)} %get-tuple-element.69, ...), channel_id=1, replica_groups=mesh['dp'=2,'space'=16] {'dp','space'}, use_global_device_ids=true, to_apply=%region_12.13 | all-reduce | flops 8448 | bytes 67584 | tf_op jit(solution)/shard_map/psum | solution.py:158
  332.3 62.0 %reduce-scatter.3.cloned.1.call-done = bf16[96,768]{1,0:T(8,128)(2,1)} async-done(((bf16[3072,768]{1,0:T(8,128)(2,1)}), bf16[96,768]{1,0:T(8,128)(2,1)}) %reduce-scatter.3.cloned.1.call-update) | async-done | bytes 147472 | tf_op jit(solution)/shard_map/reduce_scatter | solution.py:141
  394.3 1.6 multiply_bitcast_fusion
  395.9 110.6 %reduce-scatter.5.cloned.1.call-done = bf16[96,768]{1,0:T(8,128)(2,1)} async-done(((bf16[3072,768]{1,0:T(8,128)(2,1)}), bf16[96,768]{1,0:T(8,128)(2,1)}) %reduce-scatter.5.cloned.1.call-update) | async-done | bytes 147472 | tf_op jit(solution)/shard_map/reduce_scatter | solution.py:132
  506.5 1.6 convert_multiply_fusion
  (127 shorter events, 20.2 us)
Async XLA Ops:
  7.2 22.2 %all-to-all-start = ((bf16[1,16,2,8640]{3,2,0,1:T(2,128)(2,1)}), bf16[1,16,2,8640]{3,2,0,1:T(2,128)(2,1)S(1)}, u32[]{:S(2)}, u32[]{:S(2)}) async-start(bf16[1,16,2,8640]{3,2,0,1:T(2,128)(2,1)} %bitcast.227), calls=%async_computation | async-start | bytes 1114112 | tf_op jit(solution)/shard_map/all_to_all | solution.py:111
  33.4 0.9 copy-start.19
  33.4 0.9 copy-start.22
  36.5 5.0 copy-start.25
  36.5 5.2 %copy-start.26 = (f32[2,768]{1,0:T(2,128)S(1)}, f32[2,768]{1,0:T(2,128)}, u32[]{:S(2)}) copy-start(f32[2,768]{1,0:T(2,128)} %param.26) | copy-start | bytes 18436
  36.5 5.4 %copy-start.10 = (f32[2,8,96,96]{3,2,1,0:T(8,128)S(1)}, f32[2,8,96,96]{3,2,1,0:T(8,128)}, u32[]{:S(2)}) copy-start(f32[2,8,96,96]{3,2,1,0:T(8,128)} %param.23) | copy-start | bytes 1769476
  36.5 23.6 %all-to-all-start.1 = ((f32[16,2,1,2,4,768]{5,1,4,3,2,0:T(2,128)}), f32[16,2,1,2,4,768]{5,1,4,3,2,0:T(2,128)S(1)}, u32[]{:S(2)}, u32[]{:S(2)}) async-start(f32[16,2,1,2,4,768]{5,1,4,3,2,0:T(2,128)} %copy.105), calls=%async_computation.1 | async-start | bytes 1572864 | tf_op jit(solution)/shard_map/all_to_all | solution.py:70
  42.1 19.9 %copy-start.7 = (f32[1,8,96,96]{2,3,1,0:T(8,128)}, f32[1,8,96,96]{2,3,1,0:T(8,128)S(1)}, u32[]{:S(2)}) copy-start(f32[1,8,96,96]{2,3,1,0:T(8,128)S(1)} %copy.159) | copy-start | bytes 884740
  46.1 2.5 copy-start.8
  46.1 14.0 %copy-start.20 = (f32[16,2,16,2,1,1]{0,2,1,3,5,4:T(8,128)S(1)}, f32[16,2,16,2,1,1]{0,2,1,3,5,4:T(8,128)}, u32[]{:S(2)}) copy-start(f32[16,2,16,2,1,1]{0,2,1,3,5,4:T(8,128)} %constant.86) | copy-start | bytes 12292
  62.0 2.6 copy-start.4
  62.0 2.6 copy-start.9
  62.0 2.6 copy-start.16
  62.0 2.6 copy-start.17
  64.6 1.4 copy-start.11
  66.5 0.8 copy-start.24
  69.1 5.8 %copy-start.1 = (bf16[2,1,180,768]{3,0,2,1:T(2,128)(2,1)S(1)}, bf16[2,1,180,768]{3,0,2,1:T(2,128)(2,1)}, u32[]{:S(2)}) copy-start(bf16[2,1,180,768]{3,0,2,1:T(2,128)(2,1)} %param.31) | copy-start | bytes 1658884
  69.1 24.3 %all-to-all-start.2 = ((f32[16,2,1,2,4,768]{5,4,1,3,2,0:T(4,128)}), f32[16,2,1,2,4,768]{5,4,1,3,2,0:T(4,128)}, u32[]{:S(2)}, u32[]{:S(2)}) async-start(f32[16,2,1,2,4,768]{5,4,1,3,2,0:T(4,128)} %copy.118), calls=%async_computation.2 | async-start | bytes 1572864 | tf_op jit(solution)/shard_map/all_to_all | solution.py:70
  74.7 207.4 %all-reduce.12.cloned.1.call-start = ((), (), s32[]{:S(2)}) async-start(), calls=%async_computation.9 | async-start | bytes 3145728 | tf_op jit(solution)/shard_map/psum | solution.py:158
  75.1 6.7 %copy-start.14 = (bf16[360,768]{1,0:T(8,128)(2,1)}, bf16[360,768]{1,0:T(8,128)(2,1)S(1)}, u32[]{:S(2)}) copy-start(bf16[360,768]{1,0:T(8,128)(2,1)S(1)} %reshape.326) | copy-start | bytes 1658884
  75.1 18.3 %copy-start.29 = (f32[180,16,2,4,1]{0,1,3,4,2:T(8,128)S(1)}, f32[180,16,2,4,1]{0,1,3,4,2:T(8,128)}, u32[]{:S(2)}) copy-start(f32[180,16,2,4,1]{0,1,3,4,2:T(8,128)} %constant.85) | copy-start | bytes 276484
  95.8 0.7 copy-start.21
  96.5 0.7 copy-start.27
  97.2 9.6 %copy-start.15 = (bf16[360,768]{1,0:T(8,128)(2,1)}, bf16[360,768]{1,0:T(8,128)(2,1)S(1)}, u32[]{:S(2)}) copy-start(bf16[360,768]{1,0:T(8,128)(2,1)S(1)} %reshape.337) | copy-start | bytes 1658884
  106.9 1.4 copy-start.30
  114.9 1.0 copy-start
  115.9 1.8 copy-start.2
  115.9 1.8 copy-start.18
  140.4 4.4 copy-start.6
  140.4 4.4 copy-start.12
  144.7 1.2 copy-start.13
  145.7 1.1 copy-start.5
  149.9 244.3 %reduce-scatter.3.cloned.1.call-start = ((), (), s32[]{:S(2)}) async-start(), calls=%async_computation.7 | async-start | bytes 4866048 | tf_op jit(solution)/shard_map/reduce_scatter | solution.py:141
  156.5 349.9 %reduce-scatter.5.cloned.1.call-start = ((), (), s32[]{:S(2)}) async-start(), calls=%async_computation.8 | async-start | bytes 4866048 | tf_op jit(solution)/shard_map/reduce_scatter | solution.py:132
  171.4 2.5 copy-start.23
  176.6 108.2 %all-to-all-start.4 = ((bf16[16,2,1,2,4,768]{5,3,4,1,2,0:T(2,128)(2,1)}), bf16[16,2,1,2,4,768]{5,3,4,1,2,0:T(2,128)(2,1)}, u32[]{:S(2)}, u32[]{:S(2)}) async-start(bf16[16,2,1,2,4,768]{5,3,4,1,2,0:T(2,128)(2,1)} %copy.129), calls=%async_computation.4 | async-start | bytes 786432 | tf_op jit(solution)/shard_map/all_to_all | solution.py:70
  282.1 2.7 copy-start.3
  282.1 2.7 copy-start.28
Sparse Core Ops, SparseCore 0:
  150.1 132.0 all-reduce.11
  287.6 106.6 reduce-scatter.2
  399.7 106.6 reduce-scatter.4

commit v2 on v1

--- a/solution.py
+++ b/solution.py
@@ -1,9 +1,12 @@
+import functools
 import math
 
 import jax
 import jax.numpy as jnp
 import numpy as np
 from jax import lax
+from jax.experimental import pallas as pl
+from jax.experimental.pallas import tpu as pltpu
 from jax.sharding import PartitionSpec as P
 
 KW = 64
@@ -87,6 +90,113 @@
     pieces = jnp.einsum("bmked,lrcke->lbrcmd", shaped, merid, precision=high)
     modes = swap(pieces.astype(carried)).astype(jnp.float32)
     return jnp.einsum("sbrcmd,wscm->brwd", modes, zonal, precision=high)
+
+
+def total_kernel(ranks, space_ranks, scale, terms, result, landed, kept, gathered, *sems):
+    me = lax.axis_index("dp") * space_ranks + lax.axis_index("space")
+    send_term, recv_term, send_sum, recv_sum = sems
+
+    def place(peer):
+        return (peer // space_ranks, lax.rem(peer, space_ranks))
+
+    def term_copy(step):
+        peer = lax.rem(me + step, ranks)
+        return pltpu.make_async_remote_copy(
+            src_ref=terms.at[peer],
+            dst_ref=landed.at[me],
+            send_sem=send_term.at[step],
+            recv_sem=recv_term.at[step],
+            device_id=place(peer),
+            device_id_type=pl.DeviceIdType.MESH,
+        )
+
+    def sum_copy(step):
+        peer = lax.rem(me + step, ranks)
+        return pltpu.make_async_remote_copy(
+            src_ref=kept,
+            dst_ref=gathered.at[me],
+            send_sem=send_sum.at[step],
+            recv_sem=recv_sum.at[step],
+            device_id=place(peer),
+            device_id_type=pl.DeviceIdType.MESH,
+        )
+
+    barrier = pltpu.get_barrier_semaphore()
+
+    def greet(step, carry):
+        pl.semaphore_signal(
+            barrier,
+            inc=1,
+            device_id=place(lax.rem(me + step, ranks)),
+            device_id_type=pl.DeviceIdType.MESH,
+        )
+        return carry
+
+    def send_terms(step, carry):
+        term_copy(step).start()
+        return carry
+
+    def add_term(step, carry):
+        term_copy(step).wait_recv()
+        return carry + landed[lax.rem(me + ranks - step, ranks)]
+
+    def send_sums(step, carry):
+        sum_copy(step).start()
+        return carry
+
+    def finish(step, carry):
+        term_copy(step).wait_send()
+        sum_copy(step).wait()
+        return carry
+
+    lax.fori_loop(1, ranks, greet, 0)
+    pl.semaphore_wait(barrier, ranks - 1)
+    lax.fori_loop(1, ranks, send_terms, 0)
+    total = lax.fori_loop(1, ranks, add_term, terms[me]) * scale
+    kept[...] = total
+    lax.fori_loop(1, ranks, send_sums, 0)
+    lax.fori_loop(1, ranks, finish, 0)
+    gathered[me] = total
+    result[...] = gathered[...]
+
+
+def scaled_totals(parts, ranks, space_ranks, scale):
+    flat = jnp.concatenate([part.reshape(-1) for part in parts])
+    block = 8 * 128
+    rows = -(-flat.size // (ranks * block)) * 8
+    padded = jnp.pad(flat, (0, ranks * rows * 128 - flat.size)).reshape(ranks, rows, 128)
+    vmem = pl.BlockSpec(memory_space=pltpu.VMEM)
+    summed = pl.pallas_call(
+        functools.partial(total_kernel, ranks, space_ranks, scale),
+        out_shape=jax.ShapeDtypeStruct(padded.shape, jnp.float32),
+        in_specs=[vmem],
+        out_specs=vmem,
+        scratch_shapes=[
+            pltpu.VMEM(padded.shape, jnp.float32),
+            pltpu.VMEM(padded.shape[1:], jnp.float32),
+            pltpu.VMEM(padded.shape, jnp.float32),
+        ]
+        + [pltpu.SemaphoreType.DMA((ranks,))] * 4,
+        compiler_params=pltpu.CompilerParams(collective_id=0, has_side_effects=True),
+    )(padded)
+    flat_sum = summed.reshape(-1)
+    found, at = [], 0
+    for part in parts:
+        found.append(lax.slice(flat_sum, (at,), (at + part.size,)).reshape(part.shape))
+        at += part.size
+    return found
+
+
+def scattered(term, dp_ranks, space_ranks):
+    width = term.shape[-1]
+    lanes = term.reshape(dp_ranks, space_ranks, -1, width).transpose(1, 0, 2, 3)
+    rows = lanes.reshape(term.shape).astype(jnp.bfloat16)
+    return rows
+
+
+def paired(part, dp_ranks):
+    wide = part.astype(jnp.float32).reshape(dp_ranks, -1, part.shape[-1])
+    return wide
 
 
 def local(
@@ -105,6 +215,7 @@
 ):
     samples, lat_rows, lon_cells, model_width = cotangent.shape
     space_ranks = lax.axis_size("space")
+    dp_ranks = lax.axis_size("dp")
     lat_total = lat_rows * space_ranks
     tokens = samples * lat_rows * lon_cells
     blocks = spec_one.shape[1]
@@ -129,21 +240,22 @@
     active_flat = active.astype(jnp.bfloat16)
     upstream = cotangent.reshape(tokens, model_width)
     term_two = jnp.einsum("tf,td->fd", active_flat, upstream, preferred_element_type=jnp.float32)
-    part_two = lax.psum_scatter(
-        term_two.astype(jnp.bfloat16), everyone, scatter_dimension=0, tiled=True
-    )
     grad_active = jnp.einsum("td,fd->tf", upstream, fc_two, preferred_element_type=jnp.float32)
     grad_hidden = pull_gate(grad_active)[0]
     grad_hidden_flat = grad_hidden.astype(jnp.bfloat16)
     term_one = jnp.einsum(
         "tf,td->fd", grad_hidden_flat, normed_flat, preferred_element_type=jnp.float32
     )
-    part_one = lax.psum_scatter(
-        term_one.astype(jnp.bfloat16), everyone, scatter_dimension=0, tiled=True
-    )
     grad_normed_two = jnp.einsum(
         "tf,df->td", grad_hidden_flat, fc_one, preferred_element_type=jnp.float32
     )
+    rows_one = scattered(term_one, dp_ranks, space_ranks)
+    rows_two = scattered(term_two, dp_ranks, space_ranks)
+    grad_normed_two, rows_one, rows_two = lax.optimization_barrier(
+        (grad_normed_two, rows_one, rows_two)
+    )
+    part_two = lax.psum_scatter(rows_two, "space", scatter_dimension=0, tiled=True)
+    part_one = lax.psum_scatter(rows_one, "space", scatter_dimension=0, tiled=True)
     grad_mixed_norm, grad_gain_two = pull_two(grad_normed_two.reshape(mixed_field.shape))
     grad_mixed = cotangent.astype(jnp.float32) + grad_mixed_norm
     grad_spectrum = to_modes(grad_mixed, zonal_back, merid, blocks, jnp.bfloat16)
@@ -155,32 +267,37 @@
     grad_input = grad_mixed + grad_base
     bias_sum = jnp.sum(grad_hidden, axis=0)
     out_sum = jnp.sum(cotangent, axis=(0, 1, 2), dtype=jnp.float32)
-    totals = lax.psum(
+    grad_scale = 1.0 / math.sqrt(samples * dp_ranks * lat_total * lon_cells)
+    totals = scaled_totals(
         (
+            pulled[1],
+            pulled[3],
+            pulled[2],
+            pulled[4],
             grad_gain_one,
             grad_gain_two,
-            pulled[1],
-            pulled[2],
-            pulled[3],
-            pulled[4],
             bias_sum,
             out_sum,
         ),
-        everyone,
-    )
-    grad_scale = 1.0 / math.sqrt(samples * lax.axis_size("dp") * lat_total * lon_cells)
+        dp_ranks * space_ranks,
+        space_ranks,
+        grad_scale,
+    )
+    both = jnp.stack((paired(part_one, dp_ranks), paired(part_two, dp_ranks)), axis=1)
+    halves = lax.all_to_all(both, "dp", split_axis=0, concat_axis=0, tiled=True)
+    summed = jnp.sum(halves, axis=0) * grad_scale
     return (
         grad_input,
-        (part_one.astype(jnp.float32) * grad_scale).T,
-        part_two.astype(jnp.float32) * grad_scale,
-        totals[6] * grad_scale,
-        totals[7] * grad_scale,
-        totals[0] * grad_scale,
-        totals[1] * grad_scale,
-        totals[2] * grad_scale,
-        totals[3] * grad_scale,
-        totals[4] * grad_scale,
-        totals[5] * grad_scale,
+        summed[0].T,
+        summed[1],
+        totals[6],
+        totals[7],
+        totals[4],
+        totals[5],
+        totals[0],
+        totals[2],
+        totals[1],
+        totals[3],
     )
 
 

time: 521 us -> 356 us (0.68)
  waiting for transfers between devices: 310 us -> 81.4 us
  Pallas kernels: 0 us -> 75 us
  blocking collectives: 57.3 us -> 0 us
  local copies, waits for them, and re-layouts: 31.9 us -> 69.6 us
  starting transfers between devices: 22.7 us -> 32.3 us
  matrix products: 59.3 us -> 53.5 us
    reduce_scatter x2, waiting for transfers between devices: 173 us -> 27.5 us  [the longest x1 27.5 us: local(): lax.psum_scatter(rows_one, 'space', scatter_dimension=0, tiled=True)]
    psum x1 -> x0, waiting for transfers between devices: 101 us -> none  [local(): lax.psum((grad_gain_one, grad_gain_two, pulled[1], pulled[2], pulled[3],...]
    pallas_call x0 -> x1, Pallas kernels: none -> 75 us  [scaled_totals(): pl.pallas_call(functools.partial(total_kernel, ranks, space_ranks, scale)...]
    psum x1 -> x0, blocking collectives: 39.8 us -> none  [local(): lax.psum((grad_gain_one, grad_gain_two, pulled[1], pulled[2], pulled[3],...]
    all_to_all x1 -> x0, blocking collectives: 17.5 us -> none  [swap(): lax.all_to_all(pieces, 'space', split_axis=0, concat_axis=0, tiled=True)]
    convert_element_type x0 -> x4, local copies, waits for them, and re-layouts: none -> 13.6 us  [the longest x2 5.07 us: scattered(): rows = lanes.reshape(term.shape).astype(jnp.bfloat16)]
    all_to_all x3 -> x4, waiting for transfers between devices: 23.1 us -> 35.7 us  [swap(): lax.all_to_all(pieces, 'space', split_axis=0, concat_axis=0, tiled=True)]
    reshape x0 -> x8, local copies, waits for them, and re-layouts: none -> 9.51 us  [the longest x4 5.02 us: scaled_totals(): flat = jnp.concatenate([part.reshape(-1) for part in parts])]
  transfers between devices with their start and end apart: 7 -> 8, of which waited for: 6 -> 6; matrix products, arithmetic and copies ran while one was open for 11% -> 23% of each run, Pallas kernels for 0% -> 21%
where the time goes in v2:
time: 356 us; the launch traced here: 349 us
  waiting for transfers between devices  81.4 us (23%)
  Pallas kernels  75 us (21%)
  local copies, waits for them, and re-layouts  69.6 us (20%)
  matrix products  53.5 us (15%)
  starting transfers between devices  32.3 us (9%)
  other arithmetic  22.5 us (6%)
  between operations  15 us (4%)
    pallas_call x1, Pallas kernels, scaled_totals(): pl.pallas_call(functools.partial(total_kernel, ranks, space_ranks, scale)...  75 us
    all_to_all x4, waiting for transfers between devices, swap(): lax.all_to_all(pieces, 'space', split_axis=0, concat_axis=0, tiled=True)  35.7 us
    reduce_scatter x1, waiting for transfers between devices, local(): lax.psum_scatter(rows_one, 'space', scatter_dimension=0, tiled=True)  27.5 us
    all_to_all x4, starting transfers between devices, swap(): lax.all_to_all(pieces, 'space', split_axis=0, concat_axis=0, tiled=True)  19.8 us
    dot_general x6, matrix products, block_dot(): return jnp.einsum('nri,nio->nro', values, weights, precision=high)  15.5 us
    unnamed x81, local copies, waits for them, and re-layouts  15.3 us
    all_to_all x1, waiting for transfers between devices, local(): lax.all_to_all(stash, 'space', split_axis=1, concat_axis=0, tiled=True)  12.9 us
    dot_general x1, matrix products, local(): jnp.dot(normed_flat, fc_one, preferred_element_type=jnp.float32) + bias_fc  8.59 us
  transfers between devices with their start and end apart: 8, of which 6 were waited for; matrix products, arithmetic and copies ran while one was open for 23% of the time, Pallas kernels for 21%

profile of v2, /device:TPU:0, one launch (start us, length us, event | category | flops | bytes accessed | tf_op | source)
XLA Modules:
  0.0 349.3 jit_solution(1026883235664152271)
XLA Ops:
  7.2 7.4 %all-to-all-start = ((bf16[1,16,2,8640]{3,2,0,1:T(2,128)(2,1)}), bf16[1,16,2,8640]{3,2,0,1:T(2,128)(2,1)S(1)}, u32[]{:S(2)}, u32[]{:S(2)}) async-start(bf16[1,16,2,8640]{3,2,0,1:T(2,128)(2,1)} %bitcast.297), calls=%async_computation | async-start | bytes 1114112 | tf_op jit(solution)/shard_map/all_to_all | solution.py:222
  14.6 1.9 sort.17
  16.5 12.9 %all-to-all-done = bf16[1,16,2,8640]{3,2,0,1:T(2,128)(2,1)S(1)} async-done(((bf16[1,16,2,8640]{3,2,0,1:T(2,128)(2,1)}), bf16[1,16,2,8640]{3,2,0,1:T(2,128)(2,1)S(1)}, u32[]{:S(2)}, u32[]{:S(2)}) %all-to-all-start) | async-done | bytes 552992 | tf_op jit(solution)/shard_map/all_to_all | solution.py:222
  29.4 1.7 gather_fusion
  35.0 1.5 copy.115
  36.5 4.5 %all-to-all-start.1 = ((f32[16,2,1,2,4,768]{5,1,4,3,2,0:T(2,128)}), f32[16,2,1,2,4,768]{5,1,4,3,2,0:T(2,128)S(1)}, u32[]{:S(2)}, u32[]{:S(2)}) async-start(f32[16,2,1,2,4,768]{5,1,4,3,2,0:T(2,128)} %copy.115), calls=%async_computation.1 | async-start | bytes 1572864 | tf_op jit(solution)/shard_map/all_to_all | solution.py:73
  46.5 13.2 %all-to-all-done.1 = f32[16,2,1,2,4,768]{5,1,4,3,2,0:T(2,128)S(1)} async-done(((f32[16,2,1,2,4,768]{5,1,4,3,2,0:T(2,128)}), f32[16,2,1,2,4,768]{5,1,4,3,2,0:T(2,128)S(1)}, u32[]{:S(2)}, u32[]{:S(2)}) %all-to-all-start.1) | async-done | bytes 786464 | tf_op jit(solution)/shard_map/all_to_all | solution.py:73
  61.6 2.6 convolution_add_fusion.2
  68.7 5.4 %all-to-all-start.2 = ((f32[16,2,1,2,4,768]{5,4,1,3,2,0:T(4,128)}), f32[16,2,1,2,4,768]{5,4,1,3,2,0:T(4,128)}, u32[]{:S(2)}, u32[]{:S(2)}) async-start(f32[16,2,1,2,4,768]{5,4,1,3,2,0:T(4,128)} %copy.128), calls=%async_computation.2 | async-start | bytes 1572864 | tf_op jit(solution)/shard_map/all_to_all | solution.py:73
  75.6 6.3 %fusion.82 = f32[360,3072]{1,0:T(8,128)} fusion(bf16[360,768]{1,0:T(8,128)(2,1)S(1)} %reshape.358, bf16[3072,768]{1,0:T(8,128)(2,1)} %param.30), kind=kOutput, calls=%fused_computation.157 | convolution fusion | flops 1698693120 | bytes 9695232 | tf_op jit(solution)/shard_map/td,fd->tf/dot_general | solution.py:243
  81.9 11.0 %all-to-all-done.2 = f32[16,2,1,2,4,768]{5,4,1,3,2,0:T(4,128)} async-done(((f32[16,2,1,2,4,768]{5,4,1,3,2,0:T(4,128)}), f32[16,2,1,2,4,768]{5,4,1,3,2,0:T(4,128)}, u32[]{:S(2)}, u32[]{:S(2)}) %all-to-all-start.2) | async-done | bytes 786464 | tf_op jit(solution)/shard_map/all_to_all | solution.py:73
  92.9 2.4 fusion.80
  97.6 8.6 %fusion.72 = (f32[3072]{0:T(1024)S(1)}, bf16[360,3072]{1,0:T(8,128)(2,1)S(1)}, f32[360,3072]{1,0:T(8,128)S(1)}) fusion(f32[360,3072]{1,0:T(8,128)} %fusion.82, f32[3072]{0:T(1024)S(1)} %copy-done.30, bf16[360,768]{1,0:T(8,128)(2,1)} %reshape.369, bf16[768,3072]{1,0:T(8,128)(2,1)} %param.28), kind=kOutput, calls=%fused_computation.148 | convolution fusion | flops 1723020288 | bytes 16355328 | tf_op jit(solution)/shard_map/dot_general | solution.py:238
  106.2 5.2 %fusion.17 = f32[360,768]{1,0:T(8,128)} fusion(bf16[768,3072]{1,0:T(8,128)(2,1)} %param.28, bf16[360,3072]{1,0:T(8,128)(2,1)S(1)} %get-tuple-element.68), kind=kOutput, calls=%fused_computation.28 | convolution fusion | flops 1698693120 | bytes 8036352 | tf_op jit(solution)/shard_map/tf,df->td/dot_general | solution.py:249
  111.5 5.1 %fusion.13 = (bf16[3072,360]{0,1:T(8,128)(2,1)}, bf16[3072,360]{0,1:T(8,128)(2,1)}) fusion(f32[360,3072]{1,0:T(8,128)S(1)} %get-tuple-element.98, f32[360,3072]{1,0:T(8,128)S(1)} %bitcast.280), kind=kLoop, calls=%fused_computation.22 | loop fusion | flops 24330240 | bytes 13271040 | tf_op jit(solution)/shard_map/convert_element_type | solution.py:240
  116.6 4.3 %copy.130 = bf16[3072,360]{1,0:T(8,128)(2,1)} copy(bf16[3072,360]{0,1:T(8,128)(2,1)} %get-tuple-element.72) | data formatting | bytes 4423680 | tf_op jit(solution)/shard_map/convert_element_type | solution.py:245
  120.9 4.3 %convert_bitcast_fusion.1 = bf16[16,2,96,768]{3,2,0,1:T(8,128)(2,1)S(1)} fusion(bf16[2,16,96,360]{3,2,1,0:T(8,128)(2,1)} %bitcast.288, bf16[360,768,1,1]{1,0,2,3:T(8,128)(2,1)S(1)} %copy-done.16), kind=kOutput, calls=%fused_computation.6 | convolution fusion | flops 1701052416 | bytes 7483392 | tf_op jit(solution)/shard_map/tf,td->fd/dot_general | solution.py:246
  125.1 2.5 copy.131
  127.7 4.3 %copy.132 = bf16[3072,360]{1,0:T(8,128)(2,1)} copy(bf16[3072,360]{0,1:T(8,128)(2,1)} %get-tuple-element.71) | data formatting | bytes 4423680 | tf_op jit(solution)/shard_map/convert_element_type | solution.py:240
  132.0 4.3 %convert_bitcast_fusion = bf16[16,2,96,768]{3,2,0,1:T(8,128)(2,1)S(1)} fusion(bf16[2,16,96,360]{3,2,1,0:T(8,128)(2,1)} %bitcast.289, bf16[360,768,1,1]{1,0,2,3:T(8,128)(2,1)S(1)} %copy-done.15), kind=kOutput, calls=%fused_computation.5 | convolution fusion | flops 1701052416 | bytes 7483392 | tf_op jit(solution)/shard_map/tf,td->fd/dot_general | solution.py:242
  136.2 2.6 copy.133
  141.2 1.7 fusion.74
  144.6 5.4 %all-to-all-start.3 = ((bf16[16,2,1,2,4,768]{5,4,3,1,2,0:T(4,128)(2,1)}), bf16[16,2,1,2,4,768]{5,4,3,1,2,0:T(4,128)(2,1)S(1)}, u32[]{:S(2)}, u32[]{:S(2)}) async-start(bf16[16,2,1,2,4,768]{5,4,3,1,2,0:T(4,128)(2,1)} %copy.134), calls=%async_computation.3 | async-start | bytes 786432 | tf_op jit(solution)/shard_map/all_to_all | solution.py:73
  150.7 11.4 %all-to-all-done.3 = bf16[16,2,1,2,4,768]{5,4,3,1,2,0:T(4,128)(2,1)S(1)} async-done(((bf16[16,2,1,2,4,768]{5,4,3,1,2,0:T(4,128)(2,1)}), bf16[16,2,1,2,4,768]{5,4,3,1,2,0:T(4,128)(2,1)S(1)}, u32[]{:S(2)}, u32[]{:S(2)}) %all-to-all-start.3) | async-done | bytes 393248 | tf_op jit(solution)/shard_map/all_to_all | solution.py:73
  163.5 1.6 reshape.374
  166.4 4.3 %fusion.81 = (f32[8,192]{1,0:T(8,128)S(1)}, f32[8,128,192]{1,2,0:T(8,128)S(1)}) fusion(f32[8,128,192]{1,2,0:T(8,128)} %copy-done.14, f32[8,128,192]{1,2,0:T(8,128)} %bitcast.286, f32[8,96,96]{1,2,0:T(8,128)} %bitcast.300, f32[8,96,96]{1,2,0:T(8,128)} %bitcast_negate_fusion, f32[8,96,96]{1,2,0:T(8,128)} %bitcast.293), kind=kOutput, calls=%fused_computation.156 | convolution fusion | flops 231307776 | bytes 3250176 | tf_op jit(solution)/shard_map/transpose(jvp(nri,nio->nro))/dot_general | solution.py:41
  170.8 3.0 fusion.30
  173.8 2.0 fusion.83
  175.7 2.5 copy.140
  178.2 2.4 reshape.377
  180.6 1.7 fusion.23
  183.4 4.4 %all-to-all-start.4 = ((bf16[16,2,1,2,4,768]{5,3,4,1,2,0:T(2,128)(2,1)}), bf16[16,2,1,2,4,768]{5,3,4,1,2,0:T(2,128)(2,1)}, u32[]{:S(2)}, u32[]{:S(2)}) async-start(bf16[16,2,1,2,4,768]{5,3,4,1,2,0:T(2,128)(2,1)} %copy.143), calls=%async_computation.4 | async-start | bytes 786432 | tf_op jit(solution)/shard_map/all_to_all | solution.py:73
  187.8 1.9 slice_bitcast_fusion.5
  190.7 2.5 reshape.380
  193.1 2.3 fusion.55
  196.7 2.4 reshape.381
  199.1 2.0 constant_dynamic-update-slice_fusion.7
  205.0 2.2 multiply_reduce_fusion.2
  211.7 1.6 convert_reduce_fusion
  214.6 2.4 pad.36
  217.0 75.0 %shard_map.275 = f32[32,80,128]{2,1,0:T(8,128)} custom-call(f32[32,80,128]{2,1,0:T(8,128)} %bitcast.274), custom_call_target="tpu_custom_call" | custom-call | tf_op jit(solution)/shard_map/pallas_call | solution.py:169
  292.1 27.5 %reduce-scatter.3.cloned.1.call-done = bf16[192,768]{1,0:T(8,128)(2,1)} async-done(((bf16[3072,768]{1,0:T(8,128)(2,1)}), bf16[192,768]{1,0:T(8,128)(2,1)}) %reduce-scatter.3.cloned.1.call-update) | async-done | bytes 294928 | tf_op jit(solution)/shard_map/reduce_scatter | solution.py:258
  319.6 2.2 maximum_convert_fusion
  321.7 4.6 %all-to-all-start.5 = ((f32[2,2,96,768]{3,2,1,0:T(8,128)}), f32[2,2,96,768]{3,2,1,0:T(8,128)}, u32[]{:S(2)}, u32[]{:S(2)}) async-start(f32[2,2,96,768]{3,2,1,0:T(8,128)} %maximum_convert_fusion), calls=%async_computation.7 | async-start | bytes 2359296 | tf_op jit(solution)/shard_map/all_to_all | solution.py:287
  327.9 2.1 copy.148
  330.0 2.2 reshape.388
  335.1 4.8 %all-to-all-done.5 = f32[2,2,96,768]{3,2,1,0:T(8,128)} async-done(((f32[2,2,96,768]{3,2,1,0:T(8,128)}), f32[2,2,96,768]{3,2,1,0:T(8,128)}, u32[]{:S(2)}, u32[]{:S(2)}) %all-to-all-start.5) | async-done | bytes 1179680 | tf_op jit(solution)/shard_map/all_to_all | solution.py:287
  339.9 1.4 reduce_sum.146
  (157 shorter events, 44.9 us)
Async XLA Ops:
  7.2 22.2 %all-to-all-start = ((bf16[1,16,2,8640]{3,2,0,1:T(2,128)(2,1)}), bf16[1,16,2,8640]{3,2,0,1:T(2,128)(2,1)S(1)}, u32[]{:S(2)}, u32[]{:S(2)}) async-start(bf16[1,16,2,8640]{3,2,0,1:T(2,128)(2,1)} %bitcast.297), calls=%async_computation | async-start | bytes 1114112 | tf_op jit(solution)/shard_map/all_to_all | solution.py:222
  33.4 0.9 copy-start.22
  33.4 0.9 copy-start.25
  35.0 6.1 %copy-start.13 = (f32[2,8,96,96]{3,2,1,0:T(8,128)S(1)}, f32[2,8,96,96]{3,2,1,0:T(8,128)}, u32[]{:S(2)}) copy-start(f32[2,8,96,96]{3,2,1,0:T(8,128)} %param.23) | copy-start | bytes 1769476
  36.5 23.2 %all-to-all-start.1 = ((f32[16,2,1,2,4,768]{5,1,4,3,2,0:T(2,128)}), f32[16,2,1,2,4,768]{5,1,4,3,2,0:T(2,128)S(1)}, u32[]{:S(2)}, u32[]{:S(2)}) async-start(f32[16,2,1,2,4,768]{5,1,4,3,2,0:T(2,128)} %copy.115), calls=%async_computation.1 | async-start | bytes 1572864 | tf_op jit(solution)/shard_map/all_to_all | solution.py:73
  41.1 1.2 copy-start.28
  42.2 19.3 %copy-start.9 = (f32[1,8,96,96]{2,3,1,0:T(8,128)}, f32[1,8,96,96]{2,3,1,0:T(8,128)S(1)}, u32[]{:S(2)}) copy-start(f32[1,8,96,96]{2,3,1,0:T(8,128)S(1)} %copy.177) | copy-start | bytes 884740
  42.4 2.3 copy-start.29
  44.5 15.2 %copy-start.23 = (f32[16,2,16,2,1,1]{0,2,1,3,5,4:T(8,128)S(1)}, f32[16,2,16,2,1,1]{0,2,1,3,5,4:T(8,128)}, u32[]{:S(2)}) copy-start(f32[16,2,16,2,1,1]{0,2,1,3,5,4:T(8,128)} %constant.86) | copy-start | bytes 12292
  44.7 15.0 %copy-start.11 = (f32[1,8,96,96]{2,3,1,0:T(8,128)}, f32[1,8,96,96]{2,3,1,0:T(8,128)S(1)}, u32[]{:S(2)}) copy-start(f32[1,8,96,96]{2,3,1,0:T(8,128)S(1)} %copy.179) | copy-start | bytes 884740
  61.6 2.6 copy-start.6
  61.6 2.6 copy-start.12
  61.6 2.6 copy-start.18
  61.6 2.6 copy-start.20
  64.2 1.4 copy-start.14
  66.0 0.8 copy-start.27
  67.3 7.1 %copy-start.1 = (bf16[2,1,180,768]{3,0,2,1:T(2,128)(2,1)S(1)}, bf16[2,1,180,768]{3,0,2,1:T(2,128)(2,1)}, u32[]{:S(2)}) copy-start(bf16[2,1,180,768]{3,0,2,1:T(2,128)(2,1)} %param.31) | copy-start | bytes 1658884
  68.7 24.2 %all-to-all-start.2 = ((f32[16,2,1,2,4,768]{5,4,1,3,2,0:T(4,128)}), f32[16,2,1,2,4,768]{5,4,1,3,2,0:T(4,128)}, u32[]{:S(2)}, u32[]{:S(2)}) async-start(f32[16,2,1,2,4,768]{5,4,1,3,2,0:T(4,128)} %copy.128), calls=%async_computation.2 | async-start | bytes 1572864 | tf_op jit(solution)/shard_map/all_to_all | solution.py:73
  74.2 217.9 %reduce-scatter.5.cloned.1.call-start = ((), (), s32[]{:S(2)}) async-start(), calls=%async_computation.9 | async-start | bytes 5013504 | tf_op jit(solution)/shard_map/reduce_scatter | solution.py:257
  75.6 17.3 %copy-start.31 = (f32[180,16,2,4,1]{0,1,3,4,2:T(8,128)S(1)}, f32[180,16,2,4,1]{0,1,3,4,2:T(8,128)}, u32[]{:S(2)}) copy-start(f32[180,16,2,4,1]{0,1,3,4,2:T(8,128)} %constant.85) | copy-start | bytes 276484
  81.9 13.7 %copy-start.24 = (f32[768]{0:T(1024)S(1)}, f32[768]{0:T(1024)}, u32[]{:S(2)}) copy-start(f32[768]{0:T(1024)} %param.27) | copy-start | bytes 9220
  95.8 1.8 copy-start.30
  96.7 14.8 %slice-start = ((s8[4423680]{0:T(1024)(128)(4,1)}), s8[229376]{0:T(1024)(128)(4,1)S(1)}, s32[]{:S(2)}) async-start(s8[4423680]{0:T(1024)(128)(4,1)} %bitcast.279), calls=%async_computation.10 | async-start | bytes 458752
  97.6 13.8 %slice-start.1 = ((s8[4423680]{0:T(1024)(128)(4,1)}), s8[4194304]{0:T(1024)(128)(4,1)S(1)}, s32[]{:S(2)}) async-start(s8[4423680]{0:T(1024)(128)(4,1)} %bitcast.279), calls=%async_computation.11 | async-start | bytes 8388608
  116.6 4.3 %copy-start.16 = (bf16[360,768,1,1]{1,0,2,3:T(8,128)(2,1)S(1)}, bf16[360,768,1,1]{1,0,2,3:T(8,128)(2,1)}, u32[]{:S(2)}) copy-start(bf16[360,768,1,1]{1,0,2,3:T(8,128)(2,1)} %reshape.413) | copy-start | bytes 1658884
  127.7 4.3 %copy-start.15 = (bf16[360,768,1,1]{1,0,2,3:T(8,128)(2,1)S(1)}, bf16[360,768,1,1]{1,0,2,3:T(8,128)(2,1)}, u32[]{:S(2)}) copy-start(bf16[360,768,1,1]{1,0,2,3:T(8,128)(2,1)} %reshape.414) | copy-start | bytes 1658884
  140.2 1.0 copy-start
  141.2 1.8 copy-start.2
  141.2 1.8 copy-start.21
  144.6 17.5 %all-to-all-start.3 = ((bf16[16,2,1,2,4,768]{5,4,3,1,2,0:T(4,128)(2,1)}), bf16[16,2,1,2,4,768]{5,4,3,1,2,0:T(4,128)(2,1)S(1)}, u32[]{:S(2)}, u32[]{:S(2)}) async-start(bf16[16,2,1,2,4,768]{5,4,3,1,2,0:T(4,128)(2,1)} %copy.134), calls=%async_computation.3 | async-start | bytes 786432 | tf_op jit(solution)/shard_map/all_to_all | solution.py:73
  150.0 169.6 %reduce-scatter.3.cloned.1.call-start = ((), (), s32[]{:S(2)}) async-start(), calls=%async_computation.8 | async-start | bytes 5013504 | tf_op jit(solution)/shard_map/reduce_scatter | solution.py:258
  166.4 4.3 %copy-start.10 = (f32[1,8,96,96]{2,3,1,0:T(8,128)S(1)}, f32[1,8,96,96]{2,3,1,0:T(8,128)}, u32[]{:S(2)}) copy-start(f32[1,8,96,96]{2,3,1,0:T(8,128)} %copy-done.9) | copy-start | bytes 884740
  166.4 4.3 %copy-start.17 = (f32[1,8,96,96]{2,3,1,0:T(8,128)S(1)}, f32[1,8,96,96]{2,3,1,0:T(8,128)}, u32[]{:S(2)}) copy-start(f32[1,8,96,96]{2,3,1,0:T(8,128)} %copy.176) | copy-start | bytes 884740
  166.4 4.4 %copy-start.19 = (f32[8,96,96]{1,2,0:T(8,128)S(1)}, f32[8,96,96]{1,2,0:T(8,128)}, u32[]{:S(2)}) copy-start(f32[8,96,96]{1,2,0:T(8,128)} %bitcast_negate_fusion.1) | copy-start | bytes 884740
  170.7 3.0 copy-start.7
  178.2 2.4 copy-start.26
  183.4 21.6 %all-to-all-start.4 = ((bf16[16,2,1,2,4,768]{5,3,4,1,2,0:T(2,128)(2,1)}), bf16[16,2,1,2,4,768]{5,3,4,1,2,0:T(2,128)(2,1)}, u32[]{:S(2)}, u32[]{:S(2)}) async-start(bf16[16,2,1,2,4,768]{5,3,4,1,2,0:T(2,128)(2,1)} %copy.143), calls=%async_computation.4 | async-start | bytes 786432 | tf_op jit(solution)/shard_map/all_to_all | solution.py:73
  199.1 2.0 copy-start.8
  207.1 4.5 %copy-start.3 = (bf16[2,1,180,768]{3,0,2,1:T(2,128)(2,1)S(1)}, bf16[2,1,180,768]{3,0,2,1:T(2,128)(2,1)}, u32[]{:S(2)}) copy-start(bf16[2,1,180,768]{3,0,2,1:T(2,128)(2,1)} %param.31) | copy-start | bytes 1658884
  321.7 4.6 %copy-start.4 = (f32[32,80,128]{2,1,0:T(8,128)S(1)}, f32[32,80,128]{2,1,0:T(8,128)}, u32[]{:S(2)}) copy-start(f32[32,80,128]{2,1,0:T(8,128)} %shard_map.275) | copy-start | bytes 3932164
  321.7 18.2 %all-to-all-start.5 = ((f32[2,2,96,768]{3,2,1,0:T(8,128)}), f32[2,2,96,768]{3,2,1,0:T(8,128)}, u32[]{:S(2)}, u32[]{:S(2)}) async-start(f32[2,2,96,768]{3,2,1,0:T(8,128)} %maximum_convert_fusion), calls=%async_computation.7 | async-start | bytes 2359296 | tf_op jit(solution)/shard_map/all_to_all | solution.py:287
  326.3 1.5 copy-start.5
Sparse Core Ops, SparseCore 0:
  138.9 82.4 reduce-scatter.4
  225.3 94.2 reduce-scatter.2
